TPU v7x, 32 devices: a whole 2x2x4 slice. The times are simulated.
32 devices in a mesh: group: 4 (over y, x), tile: 4 (over z), video: 2 (over core).
Axes of the slice: x: 2, y: 2, z: 4, core: 2. Of those that a mesh axis runs over, the one named last changes fastest.
Arguments:
- features: bfloat16 [8, 8, 16, 24, 384], P(('video', 'tile'), 'group'), parts along dimension 0, may hold values from -6 to 6
- group_slot: int32 [4], replicated, may hold values from 0 to 3, each once
- margins: int32 [4, 4], P('tile'), may hold values from 0 to 4, as said below
- norm_gain: float32 [384], replicated, may hold values from 0.1 to 1.9
- kernel: bfloat16 [3, 3, 3, 384, 384], replicated, may hold values from -0.0625 to 0.0625
- conv_bias: float32 [384], replicated, may hold values from -3 to 3
Outputs:
- decoded: bfloat16 [8, 8, 16, 24, 384], P(('video', 'tile'), 'group'), parts along dimension 0
There are 2 independent parts, one for each index of `video`. A program takes and returns all parts, laid end to end along the dimension named above; an argument that names none is the same for every part. Nothing has to cross between parts.
Inputs may be any that keep to these rules, and one draw needn't show every extreme that they name: group_slot is a permutation of 0 to 3. margins[t] is (left, right, up, down) of tile t; a margin is 0 exactly at the image's border and 1 to 4 elsewhere; the margin a tile has toward a neighbour equals the neighbour's margin back; left and right margins depend only on the tile's column, up and down margins are the same for all columns; some margin equals 4.
All inputs are finite; a program needn't handle non-finite values.
Results may differ from a plain program's by a relative error of at most 0.0043.
Values may be sent and summed in bfloat16 or wider, within the bound.
A program may use at most 128 MiB of HBM per device.

v0:
```python
import jax
import jax.numpy as jnp
from jax import lax
from jax.sharding import PartitionSpec as P

M = 4
GRID_R = 2


def passed_along(shard, axis, by):
    peers = lax.axis_size(axis)
    pairs = [(i, i + by) for i in range(peers) if 0 <= i + by < peers]
    return lax.ppermute(shard, axis, pairs)


def activate(values, norm_gain):
    widened = values.astype(jnp.float32)
    inv_norm = lax.rsqrt(jnp.mean(widened * widened, axis=-1, keepdims=True) + 1e-06)
    return jax.nn.silu(widened * inv_norm * norm_gain).astype(jnp.bfloat16)


def convolve(padded, kernel, conv_bias, row_count, col_count):
    frame_count = padded.shape[0] - 2
    channels = padded.shape[-1]
    summed = jnp.zeros((frame_count * row_count * col_count, kernel.shape[-1]), jnp.float32)
    for tap_time in range(3):
        for tap_row in range(3):
            window = padded[tap_time : tap_time + frame_count, tap_row : tap_row + row_count]
            stacked = jnp.concatenate(
                [window[:, :, tap_col : tap_col + col_count] for tap_col in range(3)], axis=-1
            )
            flattened = stacked.reshape(frame_count * row_count * col_count, 3 * channels)
            summed = summed + jnp.dot(
                flattened,
                kernel[tap_time, tap_row].reshape(3 * channels, -1),
                preferred_element_type=jnp.float32,
            )
    return summed.reshape(frame_count, row_count, col_count, -1) + conv_bias


def window_band(core, near, far):
    position = jnp.arange(core + 2 * M, dtype=jnp.int32)
    return (position >= M - near) & (position < M + core + far)


def rim_weight(step, core, near, far):
    position = jnp.arange(core, dtype=jnp.int32)
    if step == 1:
        distance = position + 1
        margin = near
    elif step == -1:
        distance = core - position
        margin = far
    else:
        return jnp.ones((core,), jnp.float32)
    margin_f = margin.astype(jnp.float32)
    return jnp.maximum(margin_f + 1.0 - distance.astype(jnp.float32), 0.0) / (margin_f + 1.0)


def rim_source(step, core):
    if step == 1:
        return (core - M, M, 0)
    if step == -1:
        return (0, M, M + core)
    return (0, core, M)


def panel_source(step, core):
    if step == 1:
        return (M + core, M, 0)
    if step == -1:
        return (0, M, core - M)
    return (M, core, 0)


def blend_add(weighted, weight_sum, panel, step_r, step_c, row_dest, col_dest, reaches):
    core_h = weighted.shape[1]
    core_w = weighted.shape[2]
    row_len = panel.shape[1]
    col_len = panel.shape[2]
    placed = jnp.pad(
        panel.astype(jnp.float32),
        (
            (0, 0),
            (row_dest, core_h - row_dest - row_len),
            (col_dest, core_w - col_dest - col_len),
            (0, 0),
        ),
    )
    weight = (
        rim_weight(step_r, core_h, reaches[2], reaches[3])[:, None]
        * rim_weight(step_c, core_w, reaches[0], reaches[1])[None, :]
    )
    return (weighted + placed * weight[None, :, :, None], weight_sum + weight)


def gather_rims(source_block, grid_cols):
    core_h = source_block.shape[1]
    core_w = source_block.shape[2]
    result = jnp.pad(source_block, ((0, 0), (M, M), (M, M), (0, 0)))
    for step_r in (1, 0, -1):
        for step_c in (1, 0, -1):
            if step_r == 0 and step_c == 0:
                continue
            row_first, row_len, row_dest = rim_source(step_r, core_h)
            col_first, col_len, col_dest = rim_source(step_c, core_w)
            outgoing = source_block[
                :, row_first : row_first + row_len, col_first : col_first + col_len
            ]
            incoming = passed_along(outgoing, "tile", step_r * grid_cols + step_c)
            result = result.at[:, row_dest : row_dest + row_len, col_dest : col_dest + col_len].set(
                incoming
            )
    return result


def local(features, group_slot, margins, norm_gain, kernel, conv_bias):
    own_block = features[0]
    frame_count, core_h, core_w, channels = own_block.shape
    grid_cols = lax.axis_size("tile") // GRID_R
    reaches = margins[0]
    wanted = group_slot[lax.axis_index("group")] - 1
    chosen = jnp.zeros((2, core_h, core_w, channels), jnp.bfloat16)
    pieces = lax.all_gather(own_block[None], "group", axis=0, tiled=True)
    first_dev = jnp.int32(0)
    for offset in range(pieces.shape[0]):
        matches = group_slot[first_dev + offset] == wanted
        chosen = chosen + jnp.where(matches, pieces[offset], jnp.zeros_like(pieces[offset]))
    buffered = gather_rims(jnp.concatenate([chosen, own_block], axis=0), grid_cols)
    activated = activate(buffered, norm_gain)
    padded = jnp.pad(activated, ((0, 0), (1, 1), (1, 1), (0, 0)))
    weighted = jnp.zeros((frame_count, core_h, core_w, channels), jnp.float32)
    weight_sum = jnp.zeros((core_h, core_w), jnp.float32)
    inside = (
        window_band(core_h, reaches[2], reaches[3])[:, None]
        & window_band(core_w, reaches[0], reaches[1])[None, :]
    )
    inside = jnp.pad(inside, 1)
    masked = jnp.where(inside[None, :, :, None], padded, jnp.zeros_like(padded))
    outputs = convolve(masked, kernel, conv_bias, core_h + 2 * M, core_w + 2 * M).astype(
        jnp.bfloat16
    )
    for step_r in (1, 0, -1):
        for step_c in (1, 0, -1):
            row_first, row_len, row_dest = panel_source(step_r, core_h)
            col_first, col_len, col_dest = panel_source(step_c, core_w)
            outgoing = outputs[:, row_first : row_first + row_len, col_first : col_first + col_len]
            if step_r == 0 and step_c == 0:
                incoming = outgoing
            else:
                incoming = passed_along(outgoing, "tile", step_r * grid_cols + step_c)
            weighted, weight_sum = blend_add(
                weighted, weight_sum, incoming, step_r, step_c, row_dest, col_dest, reaches
            )
    return (weighted / weight_sum[None, :, :, None]).astype(jnp.bfloat16)[None]


def solution(mesh):
    return jax.shard_map(
        local,
        mesh=mesh,
        in_specs=(
            P(("video", "tile"), "group", None, None, None),
            P(),
            P("tile", None),
            P(),
            P(),
            P(),
        ),
        out_specs=P(("video", "tile"), "group", None, None, None),
        check_vma=False,
    )
```

profile of v0, /device:TPU:0, one launch (start us, length us, event | category | flops | bytes accessed | tf_op | source)
XLA Modules:
  0.0 182.1 jit_solution(15480783370561871145)
XLA Ops:
  11.4 1.5 fusion.29
  23.2 5.7 %fusion.21 = (bf16[1,1,3,384,384]{4,3,2,1,0:T(8,128)(2,1)}, bf16[1,1,3,384,384]{4,3,2,1,0:T(8,128)(2,1)}, bf16[1,1,3,384,384]{4,3,2,1,0:T(8,128)(2,1)}, bf16[1,1...) fusion(bf16[3,3,3,384,384]{4,3,2,1,0:T(8,128)(2,1)} %param.26), kind=kLoop, calls=%fused_computation.92 | loop fusion | bytes 15925248 | tf_op jit(solution)/shard_map/slice | solution.py:35
  28.9 20.4 %all-gather.2.cloned.1.call-done = bf16[4,2,16,24,384]{4,3,2,1,0:T(8,128)(2,1)} async-done(((bf16[1,2,16,24,384]{4,3,2,1,0:T(8,128)(2,1)}), bf16[4,2,16,24,384]{4,3,2,1,0:T(8,128)(2,1)}) %all-gather.2.cloned.1.call-update) | async-done | bytes 2359312 | tf_op jit(solution)/shard_map/all_gather | solution.py:124
  49.3 1.8 fusion.9
  51.3 4.3 %collective-permute-start.1 = (bf16[4,4,24,384]{3,2,1,0:T(8,128)(2,1)S(1)}, bf16[4,4,24,384]{3,2,1,0:T(8,128)(2,1)S(1)}, u32[]{:S(2)}, u32[]{:S(2)}) collective-permute-start(bf16[4,4,24,384]{3,2,1,0:T(8,128)(2,1)S(1)} %get-tuple-element.150), channel_id=1, source_target_pairs={{0,4},{2,6},{1,5},{3,7},{8,12},{10,14},{9,13},{11,15},{16,20},{18,... | collective-permute-start | bytes 884744 | tf_op jit(solution)/shard_map/ppermute | solution.py:13
  56.4 2.2 %collective-permute-start = (bf16[4,4,4,384]{3,2,1,0:T(4,128)(2,1)S(1)}, bf16[4,4,4,384]{3,2,1,0:T(4,128)(2,1)S(1)}, u32[]{:S(2)}, u32[]{:S(2)}) collective-permute-start(bf16[4,4,4,384]{3,2,1,0:T(4,128)(2,1)S(1)} %get-tuple-element.146), channel_id=1, source_target_pairs={{0,6},{1,7},{8,14},{9,15},{16,22},{17,23},{24,30},{25,31}} | collective-permute-start | bytes 147464 | tf_op jit(solution)/shard_map/ppermute | solution.py:13
  60.1 2.4 %collective-permute-start.2 = (bf16[4,4,4,384]{3,2,1,0:T(4,128)(2,1)}, bf16[4,4,4,384]{3,2,1,0:T(4,128)(2,1)}, u32[]{:S(2)}, u32[]{:S(2)}) collective-permute-start(bf16[4,4,4,384]{3,2,1,0:T(4,128)(2,1)} %get-tuple-element.147), channel_id=1, source_target_pairs={{0,2},{2,4},{4,6},{1,3},{3,5},{5,7},{8,10},{10,12},{12,14},{9,11},... | collective-permute-start | bytes 147464 | tf_op jit(solution)/shard_map/ppermute | solution.py:13
  66.0 7.2 %collective-permute-start.3 = (bf16[4,16,4,384]{3,2,1,0:T(4,128)(2,1)S(1)}, bf16[4,16,4,384]{3,2,1,0:T(4,128)(2,1)}, u32[]{:S(2)}, u32[]{:S(2)}) collective-permute-start(bf16[4,16,4,384]{3,2,1,0:T(4,128)(2,1)S(1)} %get-tuple-element.152), channel_id=1, source_target_pairs={{0,2},{2,4},{4,6},{1,3},{3,5},{5,7},{8,10},{10,12},{12,14},{9,11},... | collective-permute-start | bytes 589832 | tf_op jit(solution)/shard_map/ppermute | solution.py:13
  73.2 1.9 %dynamic-slice_select_fusion = bf16[4,4,24,384]{3,2,1,0:T(8,128)(2,1)S(1)} fusion(bf16[4,4,24,384]{3,2,1,0:T(8,128)(2,1)S(1)} %collective-permute-done.1, bf16[4,24,32,384]{3,2,1,0:T(8,128)(2,1)S(1)} %constant_dynamic-update-slice_fusion.4, s32[]{:T(128)} %bitcast.10, s32[]{:T(128)} %bitcast.11, pred[]{:T(512)} %and_reduce_fusion.1), kind=kLoop, calls=%fused_computation.58 | loop fusion | flops 147456 | bytes 884745 | tf_op jit(solution)/shard_map/select.9
  75.1 2.3 %scatter.29 = bf16[4,24,32,384]{3,2,1,0:T(8,128)(2,1)S(1)} dynamic-update-slice(bf16[4,24,32,384]{3,2,1,0:T(8,128)(2,1)S(1)} %constant_dynamic-update-slice_fusion.4, bf16[4,4,24,384]{3,2,1,0:T(8,128)(2,1)S(1)} %dynamic-slice_select_fusion, s32[]{:T(128)} %constant.276.clone.1, s32[]{:T(128)} %bitcast.10, s32[]{:T(128)} %bitcast.11, s32[]{:T(128)} %constant.276.clone.1) | dynamic-update-slice | bytes 589828 | tf_op jit(solution)/shard_map/scatter | solution.py:111
  79.0 3.4 %dynamic-slice_select_fusion.1 = bf16[4,4,4,384]{3,2,1,0:T(4,128)(2,1)} fusion(bf16[4,4,4,384]{3,2,1,0:T(4,128)(2,1)} %collective-permute-done.2, bf16[4,24,32,384]{3,2,1,0:T(8,128)(2,1)S(1)} %scatter.29, s32[]{:T(128)} %bitcast.12, s32[]{:T(128)} %bitcast.13, pred[]{:T(512)} %and_reduce_fusion), kind=kLoop, calls=%fused_computation.66 | loop fusion | flops 24576 | bytes 147465 | tf_op jit(solution)/shard_map/select.10
  82.3 2.2 %scatter.30 = bf16[4,24,32,384]{3,2,1,0:T(8,128)(2,1)S(1)} dynamic-update-slice(bf16[4,24,32,384]{3,2,1,0:T(8,128)(2,1)S(1)} %scatter.29, bf16[4,4,4,384]{3,2,1,0:T(4,128)(2,1)} %dynamic-slice_select_fusion.1, s32[]{:T(128)} %constant.276.clone.1, s32[]{:T(128)} %bitcast.12, s32[]{:T(128)} %bitcast.13, s32[]{:T(128)} %constant.276.clone.1) | dynamic-update-slice | bytes 98308 | tf_op jit(solution)/shard_map/scatter | solution.py:111
  86.6 8.5 %collective-permute-done.6 = bf16[4,4,24,384]{3,2,1,0:T(8,128)(2,1)S(1)} collective-permute-done((bf16[4,4,24,384]{3,2,1,0:T(8,128)(2,1)S(1)}, bf16[4,4,24,384]{3,2,1,0:T(8,128)(2,1)S(1)}, u32[]{:S(2)}, u32[]{:S(2)}) %collective-permute-start.6) | collective-permute-done | bytes 294944 | tf_op jit(solution)/shard_map/ppermute | solution.py:13
  97.7 2.2 %fusion.7 = bf16[4,24,32,384]{3,2,1,0:T(8,128)(2,1)S(1)} fusion(bf16[4,24,32,384]{3,2,1,0:T(8,128)(2,1)S(1)} %constant_dynamic-update-slice_fusion, f32[384]{0:T(512)} %param.25, f32[4,24,32]{2,1,0:T(8,128)S(1)} %add_rsqrt_fusion), kind=kLoop, calls=%fused_computation.9 | loop fusion | flops 9437184 | bytes 4732416 | tf_op jit(solution)/shard_map/convert_element_type | solution.py:19
  101.5 4.5 %fusion.23 = (bf16[2,24,32,384]{3,2,1,0:T(8,128)(2,1)S(1)}, bf16[2,24,32,384]{3,2,1,0:T(8,128)(2,1)S(1)}, bf16[2,24,32,384]{3,2,1,0:T(8,128)(2,1)}, bf16[2,24,32...) fusion(bf16[4,26,34,384]{3,2,1,0:T(8,128)(2,1)S(1)} %pad_select, ...), kind=kLoop, calls=%fused_computation.94 | loop fusion | bytes 18874368 | tf_op jit(solution)/shard_map/slice | solution.py:30
  105.9 6.3 %fusion.22 = (bf16[2,24,32,384]{3,2,1,0:T(8,128)(2,1)}, bf16[2,24,32,384]{3,2,1,0:T(8,128)(2,1)}, bf16[2,24,32,384]{3,2,1,0:T(8,128)(2,1)}, bf16[2,24,32,384]{3,...) fusion(bf16[4,26,34,384]{3,2,1,0:T(8,128)(2,1)S(1)} %pad_select, ...), kind=kLoop, calls=%fused_computation.93 | loop fusion | bytes 44826624 | tf_op jit(solution)/shard_map/slice | solution.py:30
  112.2 3.4 %pad_maximum_fusion = (bf16[2,24,32,1152]{3,2,1,0:T(8,128)(2,1)S(1)}, bf16[2,24,32,1152]{3,2,1,0:T(8,128)(2,1)S(1)}) fusion(bf16[2,24,32,384]{3,2,1,0:T(8,128)(2,1)} %get-tuple-element.134, bf16[2,24,32,384]{3,2,1,0:T(8,128)(2,1)} %get-tuple-element.135, bf16[2,24,32,384]{3,2,1,0:T(8,128)(2,1)} %get-tuple-element.136, ...), kind=kLoop, calls=%fused_computation.10 | loop fusion | flops 21233664 | bytes 14155776 | tf_op jit(solution)/shard_map/concatenate | solution.py:29
  115.7 2.1 %fusion.31 = f32[1536,384]{1,0:T(8,128)S(1)} fusion(bf16[1536,1152]{1,0:T(8,128)(2,1)S(1)} %bitcast.69, bf16[1152,384]{1,0:T(8,128)(2,1)S(1)} %bitcast.80), kind=kOutput, calls=%fused_computation.102 | convolution fusion | flops 1358954496 | bytes 6782976 | tf_op jit(solution)/shard_map/dot_general | solution.py:33
  117.8 3.6 %convolution_add_fusion.7 = f32[1536,384]{1,0:T(8,128)} fusion(f32[1536,384]{1,0:T(8,128)S(1)} %fusion.31, bf16[1536,1152]{1,0:T(8,128)(2,1)S(1)} %bitcast.65, bf16[1152,384]{1,0:T(8,128)(2,1)S(1)} %bitcast.79), kind=kOutput, calls=%fused_computation.27 | convolution fusion | flops 1359544320 | bytes 9142272 | tf_op jit(solution)/shard_map/dot_general | solution.py:33
  121.5 1.9 %pad_maximum_fusion.8 = bf16[2,24,32,1152]{3,2,1,0:T(8,128)(2,1)} fusion(bf16[2,24,32,384]{3,2,1,0:T(8,128)(2,1)S(1)} %copy-done.3, bf16[2,24,32,384]{3,2,1,0:T(8,128)(2,1)S(1)} %copy-done.4, bf16[2,24,32,384]{3,2,1,0:T(8,128)(2,1)S(1)} %copy-done.2), kind=kLoop, calls=%fused_computation.18 | loop fusion | flops 10616832 | bytes 7077888 | tf_op jit(solution)/shard_map/concatenate | solution.py:29
  124.6 3.9 %convolution_add_fusion.6 = f32[1536,384]{1,0:T(8,128)S(1)} fusion(f32[1536,384]{1,0:T(8,128)} %convolution_add_fusion.7, bf16[1536,1152]{1,0:T(8,128)(2,1)S(1)} %bitcast.66, bf16[1152,384]{1,0:T(8,128)(2,1)S(1)} %bitcast.78), kind=kOutput, calls=%fused_computation.26 | convolution fusion | flops 1359544320 | bytes 9142272 | tf_op jit(solution)/shard_map/dot_general | solution.py:33
  128.5 2.2 %convolution_add_fusion.5 = f32[1536,384]{1,0:T(8,128)S(1)} fusion(f32[1536,384]{1,0:T(8,128)S(1)} %convolution_add_fusion.6, bf16[1536,1152]{1,0:T(8,128)(2,1)S(1)} %bitcast.62, bf16[1152,384]{1,0:T(8,128)(2,1)S(1)} %bitcast.77), kind=kOutput, calls=%fused_computation.25 | convolution fusion | flops 1359544320 | bytes 9142272 | tf_op jit(solution)/shard_map/dot_general | solution.py:33
  131.9 2.2 %convolution_add_fusion.4 = f32[1536,384]{1,0:T(8,128)S(1)} fusion(f32[1536,384]{1,0:T(8,128)S(1)} %convolution_add_fusion.5, bf16[1536,1152]{1,0:T(8,128)(2,1)S(1)} %bitcast.67, bf16[1152,384]{1,0:T(8,128)(2,1)S(1)} %bitcast.76), kind=kOutput, calls=%fused_computation.24 | convolution fusion | flops 1359544320 | bytes 9142272 | tf_op jit(solution)/shard_map/dot_general | solution.py:33
  134.0 2.1 %convolution_add_fusion.3 = f32[1536,384]{1,0:T(8,128)S(1)} fusion(f32[1536,384]{1,0:T(8,128)S(1)} %convolution_add_fusion.4, bf16[1536,1152]{1,0:T(8,128)(2,1)S(1)} %bitcast.63, bf16[1152,384]{1,0:T(8,128)(2,1)S(1)} %bitcast.75), kind=kOutput, calls=%fused_computation.23 | convolution fusion | flops 1359544320 | bytes 9142272 | tf_op jit(solution)/shard_map/dot_general | solution.py:33
  137.4 2.2 %convolution_add_fusion.2 = f32[1536,384]{1,0:T(8,128)S(1)} fusion(f32[1536,384]{1,0:T(8,128)S(1)} %convolution_add_fusion.3, bf16[1536,1152]{1,0:T(8,128)(2,1)S(1)} %bitcast.68, bf16[1152,384]{1,0:T(8,128)(2,1)S(1)} %bitcast.74), kind=kOutput, calls=%fused_computation.22 | convolution fusion | flops 1359544320 | bytes 9142272 | tf_op jit(solution)/shard_map/dot_general | solution.py:33
  139.6 2.1 %convolution_add_fusion.1 = f32[1536,384]{1,0:T(8,128)S(1)} fusion(f32[1536,384]{1,0:T(8,128)S(1)} %convolution_add_fusion.2, bf16[1536,1152]{1,0:T(8,128)(2,1)S(1)} %bitcast.64, bf16[1152,384]{1,0:T(8,128)(2,1)S(1)} %bitcast.73), kind=kOutput, calls=%fused_computation.21 | convolution fusion | flops 1359544320 | bytes 9142272 | tf_op jit(solution)/shard_map/dot_general | solution.py:33
  141.8 2.1 %convolution_add_fusion = f32[1536,384]{1,0:T(8,128)S(1)} fusion(f32[1536,384]{1,0:T(8,128)S(1)} %convolution_add_fusion.1, bf16[1536,1152]{1,0:T(8,128)(2,1)S(1)} %bitcast.70, bf16[1152,384]{1,0:T(8,128)(2,1)S(1)} %bitcast.72), kind=kOutput, calls=%fused_computation.20 | convolution fusion | flops 1359544320 | bytes 9142272 | tf_op jit(solution)/shard_map/dot_general | solution.py:33
  148.4 4.5 %collective-permute-start.10 = (bf16[2,4,4,384]{3,2,1,0:T(4,128)(2,1)S(1)}, bf16[2,4,4,384]{3,2,1,0:T(4,128)(2,1)S(1)}, u32[]{:S(2)}, u32[]{:S(2)}) collective-permute-start(bf16[2,4,4,384]{3,2,1,0:T(4,128)(2,1)S(1)} %get-tuple-element.140), channel_id=1, source_target_pairs={{0,2},{2,4},{4,6},{1,3},{3,5},{5,7},{8,10},{10,12},{12,14},{9,11},... | collective-permute-start | bytes 73736 | tf_op jit(solution)/shard_map/ppermute | solution.py:13
  152.9 1.9 %collective-permute-start.11 = (bf16[2,16,4,384]{3,2,1,0:T(4,128)(2,1)S(1)}, bf16[2,16,4,384]{3,2,1,0:T(4,128)(2,1)S(1)}, u32[]{:S(2)}, u32[]{:S(2)}) collective-permute-start(bf16[2,16,4,384]{3,2,1,0:T(4,128)(2,1)S(1)} %get-tuple-element.143), channel_id=1, source_target_pairs={{0,2},{2,4},{4,6},{1,3},{3,5},{5,7},{8,10},{10,12},{12,14},{9,11},... | collective-permute-start | bytes 294920 | tf_op jit(solution)/shard_map/ppermute | solution.py:13
  156.2 6.9 %collective-permute-start.9 = (bf16[2,4,24,384]{3,2,1,0:T(8,128)(2,1)S(1)}, bf16[2,4,24,384]{3,2,1,0:T(8,128)(2,1)S(1)}, u32[]{:S(2)}, u32[]{:S(2)}) collective-permute-start(bf16[2,4,24,384]{3,2,1,0:T(8,128)(2,1)S(1)} %get-tuple-element.141), channel_id=1, source_target_pairs={{0,4},{2,6},{1,5},{3,7},{8,12},{10,14},{9,13},{11,15},{16,20},{18,... | collective-permute-start | bytes 442376 | tf_op jit(solution)/shard_map/ppermute | solution.py:13
  165.7 7.4 %collective-permute-done.14 = bf16[2,4,24,384]{3,2,1,0:T(8,128)(2,1)S(1)} collective-permute-done((bf16[2,4,24,384]{3,2,1,0:T(8,128)(2,1)S(1)}, bf16[2,4,24,384]{3,2,1,0:T(8,128)(2,1)S(1)}, u32[]{:S(2)}, u32[]{:S(2)}) %collective-permute-start.14) | collective-permute-done | bytes 147488 | tf_op jit(solution)/shard_map/ppermute | solution.py:13
  173.1 2.1 %fusion.12 = bf16[1,2,16,24,384]{4,3,2,1,0:T(8,128)(2,1)} fusion(f32[16,24]{1,0:T(8,128)S(1)} %get-tuple-element.154, f32[16,24]{1,0:T(8,128)S(1)} %get-tuple-element.155, bf16[2,4,4,384]{3,2,1,0:T(4,128)(2,1)S(1)} %collective-permute-done.15, f32[16]{0:T(128)S(1)} %get-tuple-element.179, bf16[2,4,24,384]{3,2,1,0:T(8,128)(2,1)S(1)} %collective-permute-done.14, ...), kind=kLoop, calls=%fused_computation.55 | loop fusion | flops 7962624 | bytes 1777472 | tf_op jit(solution)/shard_map/broadcast_in_dim | solution.py:155
  (94 shorter events, 32.2 us)
Async XLA Ops:
  6.5 42.7 %all-gather.2.cloned.1.call-start = ((), (), s32[]{:S(2)}) async-start(), calls=%async_computation | async-start | bytes 2949120 | tf_op jit(solution)/shard_map/all_gather | solution.py:124
  28.8 22.2 %copy-start = (bf16[1,2,16,24,384]{4,3,2,1,0:T(8,128)(2,1)S(1)}, bf16[1,2,16,24,384]{4,3,2,1,0:T(8,128)(2,1)}, u32[]{:S(2)}) copy-start(bf16[1,2,16,24,384]{4,3,2,1,0:T(8,128)(2,1)} %param.22) | copy-start | bytes 1769476
  51.3 14.7 %collective-permute-start.1 = (bf16[4,4,24,384]{3,2,1,0:T(8,128)(2,1)S(1)}, bf16[4,4,24,384]{3,2,1,0:T(8,128)(2,1)S(1)}, u32[]{:S(2)}, u32[]{:S(2)}) collective-permute-start(bf16[4,4,24,384]{3,2,1,0:T(8,128)(2,1)S(1)} %get-tuple-element.150), channel_id=1, source_target_pairs={{0,4},{2,6},{1,5},{3,7},{8,12},{10,14},{9,13},{11,15},{16,20},{18,... | collective-permute-start | bytes 884744 | tf_op jit(solution)/shard_map/ppermute | solution.py:13
  56.4 8.3 %collective-permute-start = (bf16[4,4,4,384]{3,2,1,0:T(4,128)(2,1)S(1)}, bf16[4,4,4,384]{3,2,1,0:T(4,128)(2,1)S(1)}, u32[]{:S(2)}, u32[]{:S(2)}) collective-permute-start(bf16[4,4,4,384]{3,2,1,0:T(4,128)(2,1)S(1)} %get-tuple-element.146), channel_id=1, source_target_pairs={{0,6},{1,7},{8,14},{9,15},{16,22},{17,23},{24,30},{25,31}} | collective-permute-start | bytes 147464 | tf_op jit(solution)/shard_map/ppermute | solution.py:13
  58.8 37.5 %collective-permute-start.7 = (bf16[4,4,4,384]{3,2,1,0:T(4,128)(2,1)}, bf16[4,4,4,384]{3,2,1,0:T(4,128)(2,1)}, u32[]{:S(2)}, u32[]{:S(2)}) collective-permute-start(bf16[4,4,4,384]{3,2,1,0:T(4,128)(2,1)} %get-tuple-element.145), channel_id=1, source_target_pairs={{6,0},{7,1},{14,8},{15,9},{22,16},{23,17},{30,24},{31,25}} | collective-permute-start | bytes 147464 | tf_op jit(solution)/shard_map/ppermute | solution.py:13
  60.1 17.4 %collective-permute-start.2 = (bf16[4,4,4,384]{3,2,1,0:T(4,128)(2,1)}, bf16[4,4,4,384]{3,2,1,0:T(4,128)(2,1)}, u32[]{:S(2)}, u32[]{:S(2)}) collective-permute-start(bf16[4,4,4,384]{3,2,1,0:T(4,128)(2,1)} %get-tuple-element.147), channel_id=1, source_target_pairs={{0,2},{2,4},{4,6},{1,3},{3,5},{5,7},{8,10},{10,12},{12,14},{9,11},... | collective-permute-start | bytes 147464 | tf_op jit(solution)/shard_map/ppermute | solution.py:13
  62.5 23.3 %collective-permute-start.5 = (bf16[4,4,4,384]{3,2,1,0:T(4,128)(2,1)}, bf16[4,4,4,384]{3,2,1,0:T(4,128)(2,1)}, u32[]{:S(2)}, u32[]{:S(2)}) collective-permute-start(bf16[4,4,4,384]{3,2,1,0:T(4,128)(2,1)} %get-tuple-element.148), channel_id=1, source_target_pairs={{2,0},{4,2},{6,4},{3,1},{5,3},{7,5},{10,8},{12,10},{14,12},{11,9},... | collective-permute-start | bytes 147464 | tf_op jit(solution)/shard_map/ppermute | solution.py:13
  64.6 21.0 %collective-permute-start.4 = (bf16[4,16,4,384]{3,2,1,0:T(4,128)(2,1)S(1)}, bf16[4,16,4,384]{3,2,1,0:T(4,128)(2,1)S(1)}, u32[]{:S(2)}, u32[]{:S(2)}) collective-permute-start(bf16[4,16,4,384]{3,2,1,0:T(4,128)(2,1)S(1)} %get-tuple-element.151), channel_id=1, source_target_pairs={{2,0},{4,2},{6,4},{3,1},{5,3},{7,5},{10,8},{12,10},{14,12},{11,9},... | collective-permute-start | bytes 589832 | tf_op jit(solution)/shard_map/ppermute | solution.py:13
  66.0 18.6 %collective-permute-start.3 = (bf16[4,16,4,384]{3,2,1,0:T(4,128)(2,1)S(1)}, bf16[4,16,4,384]{3,2,1,0:T(4,128)(2,1)}, u32[]{:S(2)}, u32[]{:S(2)}) collective-permute-start(bf16[4,16,4,384]{3,2,1,0:T(4,128)(2,1)S(1)} %get-tuple-element.152), channel_id=1, source_target_pairs={{0,2},{2,4},{4,6},{1,3},{3,5},{5,7},{8,10},{10,12},{12,14},{9,11},... | collective-permute-start | bytes 589832 | tf_op jit(solution)/shard_map/ppermute | solution.py:13
  77.5 17.6 %collective-permute-start.6 = (bf16[4,4,24,384]{3,2,1,0:T(8,128)(2,1)S(1)}, bf16[4,4,24,384]{3,2,1,0:T(8,128)(2,1)S(1)}, u32[]{:S(2)}, u32[]{:S(2)}) collective-permute-start(bf16[4,4,24,384]{3,2,1,0:T(8,128)(2,1)S(1)} %get-tuple-element.149), channel_id=1, source_target_pairs={{4,0},{6,2},{5,1},{7,3},{12,8},{14,10},{13,9},{15,11},{20,16},{22,... | collective-permute-start | bytes 884744 | tf_op jit(solution)/shard_map/ppermute | solution.py:13
  112.2 3.4 %copy-start.14 = (bf16[1,1,3,384,384]{4,3,2,1,0:T(8,128)(2,1)S(1)}, bf16[1,1,3,384,384]{4,3,2,1,0:T(8,128)(2,1)}, u32[]{:S(2)}) copy-start(bf16[1,1,3,384,384]{4,3,2,1,0:T(8,128)(2,1)} %get-tuple-element.108) | copy-start | bytes 2654212
  115.7 2.1 %copy-start.13 = (bf16[1,1,3,384,384]{4,3,2,1,0:T(8,128)(2,1)S(1)}, bf16[1,1,3,384,384]{4,3,2,1,0:T(8,128)(2,1)}, u32[]{:S(2)}) copy-start(bf16[1,1,3,384,384]{4,3,2,1,0:T(8,128)(2,1)} %get-tuple-element.107) | copy-start | bytes 2654212
  117.8 3.7 %copy-start.2 = (bf16[2,24,32,384]{3,2,1,0:T(8,128)(2,1)S(1)}, bf16[2,24,32,384]{3,2,1,0:T(8,128)(2,1)}, u32[]{:S(2)}) copy-start(bf16[2,24,32,384]{3,2,1,0:T(8,128)(2,1)} %get-tuple-element.110) | copy-start | bytes 3538948
  117.8 3.7 %copy-start.3 = (bf16[2,24,32,384]{3,2,1,0:T(8,128)(2,1)S(1)}, bf16[2,24,32,384]{3,2,1,0:T(8,128)(2,1)}, u32[]{:S(2)}) copy-start(bf16[2,24,32,384]{3,2,1,0:T(8,128)(2,1)} %get-tuple-element.111) | copy-start | bytes 3538948
  117.8 3.7 %copy-start.4 = (bf16[2,24,32,384]{3,2,1,0:T(8,128)(2,1)S(1)}, bf16[2,24,32,384]{3,2,1,0:T(8,128)(2,1)}, u32[]{:S(2)}) copy-start(bf16[2,24,32,384]{3,2,1,0:T(8,128)(2,1)} %get-tuple-element.112) | copy-start | bytes 3538948
  121.5 1.9 %copy-start.1 = (bf16[2,24,32,384]{3,2,1,0:T(8,128)(2,1)S(1)}, bf16[2,24,32,384]{3,2,1,0:T(8,128)(2,1)}, u32[]{:S(2)}) copy-start(bf16[2,24,32,384]{3,2,1,0:T(8,128)(2,1)} %get-tuple-element.128) | copy-start | bytes 3538948
  124.6 4.0 %copy-start.11 = (bf16[1,1,3,384,384]{4,3,2,1,0:T(8,128)(2,1)S(1)}, bf16[1,1,3,384,384]{4,3,2,1,0:T(8,128)(2,1)}, u32[]{:S(2)}) copy-start(bf16[1,1,3,384,384]{4,3,2,1,0:T(8,128)(2,1)} %get-tuple-element.105) | copy-start | bytes 2654212
  130.7 1.2 copy-start.10
  131.9 2.2 %copy-start.9 = (bf16[1,1,3,384,384]{4,3,2,1,0:T(8,128)(2,1)S(1)}, bf16[1,1,3,384,384]{4,3,2,1,0:T(8,128)(2,1)}, u32[]{:S(2)}) copy-start(bf16[1,1,3,384,384]{4,3,2,1,0:T(8,128)(2,1)} %get-tuple-element.103) | copy-start | bytes 2654212
  137.4 2.2 %copy-start.7 = (bf16[1,1,3,384,384]{4,3,2,1,0:T(8,128)(2,1)S(1)}, bf16[1,1,3,384,384]{4,3,2,1,0:T(8,128)(2,1)}, u32[]{:S(2)}) copy-start(bf16[1,1,3,384,384]{4,3,2,1,0:T(8,128)(2,1)} %get-tuple-element.109) | copy-start | bytes 2654212
  139.6 2.1 %copy-start.5 = (bf16[2,24,32,1152]{3,2,1,0:T(8,128)(2,1)S(1)}, bf16[2,24,32,1152]{3,2,1,0:T(8,128)(2,1)}, u32[]{:S(2)}) copy-start(bf16[2,24,32,1152]{3,2,1,0:T(8,128)(2,1)} %pad_maximum_fusion.8) | copy-start | bytes 10616836
  139.6 2.2 %copy-start.6 = (bf16[1,1,3,384,384]{4,3,2,1,0:T(8,128)(2,1)S(1)}, bf16[1,1,3,384,384]{4,3,2,1,0:T(8,128)(2,1)}, u32[]{:S(2)}) copy-start(bf16[1,1,3,384,384]{4,3,2,1,0:T(8,128)(2,1)} %get-tuple-element.101) | copy-start | bytes 2654212
  141.8 2.1 %copy-start.16 = (f32[384]{0:T(512)S(1)}, f32[384]{0:T(512)}, u32[]{:S(2)}) copy-start(f32[384]{0:T(512)} %param.27) | copy-start | bytes 4612
  143.9 20.5 %copy-start.15 = (f32[24]{0:T(128)S(1)}, f32[24]{0:T(128)}, u32[]{:S(2)}) copy-start(f32[24]{0:T(128)} %get-tuple-element.182) | copy-start | bytes 292
  144.4 10.5 %collective-permute-start.8 = (bf16[2,4,4,384]{3,2,1,0:T(4,128)(2,1)S(1)}, bf16[2,4,4,384]{3,2,1,0:T(4,128)(2,1)S(1)}, u32[]{:S(2)}, u32[]{:S(2)}) collective-permute-start(bf16[2,4,4,384]{3,2,1,0:T(4,128)(2,1)S(1)} %get-tuple-element.137), channel_id=1, source_target_pairs={{0,6},{1,7},{8,14},{9,15},{16,22},{17,23},{24,30},{25,31}} | collective-permute-start | bytes 73736 | tf_op jit(solution)/shard_map/ppermute | solution.py:13
  145.7 10.5 %collective-permute-start.15 = (bf16[2,4,4,384]{3,2,1,0:T(4,128)(2,1)S(1)}, bf16[2,4,4,384]{3,2,1,0:T(4,128)(2,1)S(1)}, u32[]{:S(2)}, u32[]{:S(2)}) collective-permute-start(bf16[2,4,4,384]{3,2,1,0:T(4,128)(2,1)S(1)} %get-tuple-element.138), channel_id=1, source_target_pairs={{6,0},{7,1},{14,8},{15,9},{22,16},{23,17},{30,24},{31,25}} | collective-permute-start | bytes 73736 | tf_op jit(solution)/shard_map/ppermute | solution.py:13
  147.0 16.1 %collective-permute-start.13 = (bf16[2,4,4,384]{3,2,1,0:T(4,128)(2,1)S(1)}, bf16[2,4,4,384]{3,2,1,0:T(4,128)(2,1)S(1)}, u32[]{:S(2)}, u32[]{:S(2)}) collective-permute-start(bf16[2,4,4,384]{3,2,1,0:T(4,128)(2,1)S(1)} %get-tuple-element.139), channel_id=1, source_target_pairs={{2,0},{4,2},{6,4},{3,1},{5,3},{7,5},{10,8},{12,10},{14,12},{11,9},... | collective-permute-start | bytes 73736 | tf_op jit(solution)/shard_map/ppermute | solution.py:13
  148.4 16.1 %collective-permute-start.10 = (bf16[2,4,4,384]{3,2,1,0:T(4,128)(2,1)S(1)}, bf16[2,4,4,384]{3,2,1,0:T(4,128)(2,1)S(1)}, u32[]{:S(2)}, u32[]{:S(2)}) collective-permute-start(bf16[2,4,4,384]{3,2,1,0:T(4,128)(2,1)S(1)} %get-tuple-element.140), channel_id=1, source_target_pairs={{0,2},{2,4},{4,6},{1,3},{3,5},{5,7},{8,10},{10,12},{12,14},{9,11},... | collective-permute-start | bytes 73736 | tf_op jit(solution)/shard_map/ppermute | solution.py:13
  152.9 11.6 %collective-permute-start.11 = (bf16[2,16,4,384]{3,2,1,0:T(4,128)(2,1)S(1)}, bf16[2,16,4,384]{3,2,1,0:T(4,128)(2,1)S(1)}, u32[]{:S(2)}, u32[]{:S(2)}) collective-permute-start(bf16[2,16,4,384]{3,2,1,0:T(4,128)(2,1)S(1)} %get-tuple-element.143), channel_id=1, source_target_pairs={{0,2},{2,4},{4,6},{1,3},{3,5},{5,7},{8,10},{10,12},{12,14},{9,11},... | collective-permute-start | bytes 294920 | tf_op jit(solution)/shard_map/ppermute | solution.py:13
  154.9 9.6 %collective-permute-start.12 = (bf16[2,16,4,384]{3,2,1,0:T(4,128)(2,1)S(1)}, bf16[2,16,4,384]{3,2,1,0:T(4,128)(2,1)S(1)}, u32[]{:S(2)}, u32[]{:S(2)}) collective-permute-start(bf16[2,16,4,384]{3,2,1,0:T(4,128)(2,1)S(1)} %get-tuple-element.144), channel_id=1, source_target_pairs={{2,0},{4,2},{6,4},{3,1},{5,3},{7,5},{10,8},{12,10},{14,12},{11,9},... | collective-permute-start | bytes 294920 | tf_op jit(solution)/shard_map/ppermute | solution.py:13
  156.2 9.6 %collective-permute-start.9 = (bf16[2,4,24,384]{3,2,1,0:T(8,128)(2,1)S(1)}, bf16[2,4,24,384]{3,2,1,0:T(8,128)(2,1)S(1)}, u32[]{:S(2)}, u32[]{:S(2)}) collective-permute-start(bf16[2,4,24,384]{3,2,1,0:T(8,128)(2,1)S(1)} %get-tuple-element.141), channel_id=1, source_target_pairs={{0,4},{2,6},{1,5},{3,7},{8,12},{10,14},{9,13},{11,15},{16,20},{18,... | collective-permute-start | bytes 442376 | tf_op jit(solution)/shard_map/ppermute | solution.py:13
  163.1 10.0 %collective-permute-start.14 = (bf16[2,4,24,384]{3,2,1,0:T(8,128)(2,1)S(1)}, bf16[2,4,24,384]{3,2,1,0:T(8,128)(2,1)S(1)}, u32[]{:S(2)}, u32[]{:S(2)}) collective-permute-start(bf16[2,4,24,384]{3,2,1,0:T(8,128)(2,1)S(1)} %get-tuple-element.142), channel_id=1, source_target_pairs={{4,0},{6,2},{5,1},{7,3},{12,8},{14,10},{13,9},{15,11},{20,16},{22,... | collective-permute-start | bytes 442376 | tf_op jit(solution)/shard_map/ppermute | solution.py:13
  (2 other events, 2.3 us)
Sparse Core Ops, SparseCore 0:
  9.2 40.0 all-gather.1
where the time goes:
time: 183 us; the launch traced here: 182 us
  starting transfers between devices  41.4 us (23%)
  waiting for transfers between devices  38.2 us (21%)
  local copies, waits for them, and re-layouts  31.3 us (17%)
  other arithmetic  26.4 us (14%)
  matrix products  22.5 us (12%)
  between operations  22.2 us (12%)
    ppermute x16, starting transfers between devices, passed_along(): return lax.ppermute(shard, axis, pairs)  41.4 us
    dot_general x9, matrix products, convolve(): jnp.dot(flattened, kernel[tap_time, tap_row].reshape(3 * channels, -1), p...  22.5 us
    all_gather x1, waiting for transfers between devices, local(): pieces = lax.all_gather(own_block[None], 'group', axis=0, tiled=True)  20.4 us
    ppermute x16, waiting for transfers between devices, passed_along(): return lax.ppermute(shard, axis, pairs)  17.1 us
    slice x2, local copies, waits for them, and re-layouts, convolve(): window[:, :, tap_col:tap_col + col_count]  10.8 us
    scatter x8, local copies, waits for them, and re-layouts, gather_rims(): result.at[:, row_dest:row_dest + row_len, col_dest:col_dest + col_len]  8.67 us
    another operation x6, other arithmetic  8.1 us
    concatenate x5, other arithmetic, convolve(): jnp.concatenate([window[:, :, tap_col:tap_col + col_count] for tap_col in...  8 us
  transfers between devices with their start and end apart: 17, of which 4 were waited for; matrix products, arithmetic and copies ran while one was open for 16% of the time, Pallas kernels for 0%

commit v1 on v0

--- a/solution.py
+++ b/solution.py
@@ -121,7 +121,15 @@
     reaches = margins[0]
     wanted = group_slot[lax.axis_index("group")] - 1
     chosen = jnp.zeros((2, core_h, core_w, channels), jnp.bfloat16)
-    pieces = lax.all_gather(own_block[None], "group", axis=0, tiled=True)
+    ways, here = (lax.axis_size("group"), lax.axis_index("group"))
+    grown, reach = (own_block[None], 1)
+    while reach < ways:
+        theirs = lax.ppermute(grown, "group", [(d, d ^ reach) for d in range(ways)])
+        mine_first = jnp.concatenate([grown, theirs], axis=0)
+        theirs_first = jnp.concatenate([theirs, grown], axis=0)
+        grown = jnp.where(here & reach == 0, mine_first, theirs_first)
+        reach = 2 * reach
+    pieces = grown
     first_dev = jnp.int32(0)
     for offset in range(pieces.shape[0]):
         matches = group_slot[first_dev + offset] == wanted

time: 183 us -> 171 us (0.934)
  between operations: 22.2 us -> 8.72 us
  starting transfers between devices: 41.4 us -> 45 us
  waiting for transfers between devices: 38.2 us -> 35.7 us
    all_gather x1 -> x0, waiting for transfers between devices: 20.4 us -> none  [local(): pieces = lax.all_gather(own_block[None], 'group', axis=0, tiled=True)]
    ppermute x0 -> x2, waiting for transfers between devices: none -> 18.9 us  [local(): theirs = lax.ppermute(grown, 'group', [(d, d ^ reach) for d in range(ways)])]
    ppermute x0 -> x2, starting transfers between devices: none -> 4.8 us  [local(): theirs = lax.ppermute(grown, 'group', [(d, d ^ reach) for d in range(ways)])]
    select_n x0 -> x2, other arithmetic: none -> 1.9 us  [local(): grown = jnp.where(here & reach == 0, mine_first, theirs_first)]
  transfers between devices with their start and end apart: 17 -> 18, of which waited for: 4 -> 5; matrix products, arithmetic and copies ran while one was open for 16% -> 16% of each run, Pallas kernels for 0% -> 0%
where the time goes in v1:
time: 171 us; the launch traced here: 170 us
  starting transfers between devices  45 us (26%)
  waiting for transfers between devices  35.7 us (21%)
  local copies, waits for them, and re-layouts  32.4 us (19%)
  other arithmetic  25.4 us (15%)
  matrix products  22.5 us (13%)
  between operations  8.72 us (5%)
    ppermute x16, starting transfers between devices, passed_along(): return lax.ppermute(shard, axis, pairs)  40.2 us
    dot_general x9, matrix products, convolve(): jnp.dot(flattened, kernel[tap_time, tap_row].reshape(3 * channels, -1), p...  22.5 us
    ppermute x2, waiting for transfers between devices, local(): theirs = lax.ppermute(grown, 'group', [(d, d ^ reach) for d in range(ways)])  18.9 us
    ppermute x16, waiting for transfers between devices, passed_along(): return lax.ppermute(shard, axis, pairs)  16.9 us
    slice x2, local copies, waits for them, and re-layouts, convolve(): window[:, :, tap_col:tap_col + col_count]  10.8 us
    scatter x8, local copies, waits for them, and re-layouts, gather_rims(): result.at[:, row_dest:row_dest + row_len, col_dest:col_dest + col_len]  8.9 us
    concatenate x5, other arithmetic, convolve(): jnp.concatenate([window[:, :, tap_col:tap_col + col_count] for tap_col in...  7.99 us
    another operation x6, other arithmetic  6.82 us
  transfers between devices with their start and end apart: 18, of which 5 were waited for; matrix products, arithmetic and copies ran while one was open for 16% of the time, Pallas kernels for 0%

profile of v1, /device:TPU:0, one launch (start us, length us, event | category | flops | bytes accessed | tf_op | source)
XLA Modules:
  0.0 169.8 jit_solution(3794315833412526676)
XLA Ops:
  0.0 3.0 %collective-permute-start = (bf16[1,2,16,24,384]{4,3,2,1,0:T(8,128)(2,1)}, bf16[1,2,16,24,384]{4,3,2,1,0:T(8,128)(2,1)S(1)}, u32[]{:S(2)}, u32[]{:S(2)}) collective-permute-start(bf16[1,2,16,24,384]{4,3,2,1,0:T(8,128)(2,1)} %param.22), channel_id=1, source_target_pairs={{0,8},{8,0},{16,24},{24,16},{1,9},{9,1},{17,25},{25,17},{2,10},{10... | collective-permute-start | bytes 1769480 | tf_op jit(solution)/shard_map/ppermute | solution.py:127
  14.2 2.3 %collective-permute-done = bf16[1,2,16,24,384]{4,3,2,1,0:T(8,128)(2,1)S(1)} collective-permute-done((bf16[1,2,16,24,384]{4,3,2,1,0:T(8,128)(2,1)}, bf16[1,2,16,24,384]{4,3,2,1,0:T(8,128)(2,1)S(1)}, u32[]{:S(2)}, u32[]{:S(2)}) %collective-permute-start) | collective-permute-done | bytes 589856 | tf_op jit(solution)/shard_map/ppermute | solution.py:127
  23.0 5.6 %fusion.21 = (bf16[1,1,3,384,384]{4,3,2,1,0:T(8,128)(2,1)}, bf16[1,1,3,384,384]{4,3,2,1,0:T(8,128)(2,1)}, bf16[1,1,3,384,384]{4,3,2,1,0:T(8,128)(2,1)}, bf16[1,1...) fusion(bf16[3,3,3,384,384]{4,3,2,1,0:T(8,128)(2,1)} %param.26), kind=kLoop, calls=%fused_computation.94 | loop fusion | bytes 15925248 | tf_op jit(solution)/shard_map/slice | solution.py:35
  28.6 16.5 %collective-permute-done.1 = bf16[2,2,16,24,384]{4,3,2,1,0:T(8,128)(2,1)S(1)} collective-permute-done((bf16[2,2,16,24,384]{4,3,2,1,0:T(8,128)(2,1)S(1)}, bf16[2,2,16,24,384]{4,3,2,1,0:T(8,128)(2,1)S(1)}, u32[]{:S(2)}, u32[]{:S(2)}) %collective-permute-start.1) | collective-permute-done | bytes 1179680 | tf_op jit(solution)/shard_map/ppermute | solution.py:127
  46.9 4.5 %collective-permute-start.3 = (bf16[4,4,24,384]{3,2,1,0:T(8,128)(2,1)S(1)}, bf16[4,4,24,384]{3,2,1,0:T(8,128)(2,1)S(1)}, u32[]{:S(2)}, u32[]{:S(2)}) collective-permute-start(bf16[4,4,24,384]{3,2,1,0:T(8,128)(2,1)S(1)} %get-tuple-element.150), channel_id=1, source_target_pairs={{0,4},{2,6},{1,5},{3,7},{8,12},{10,14},{9,13},{11,15},{16,20},{18,... | collective-permute-start | bytes 884744 | tf_op jit(solution)/shard_map/ppermute | solution.py:13
  52.1 2.3 %collective-permute-start.2 = (bf16[4,4,4,384]{3,2,1,0:T(4,128)(2,1)S(1)}, bf16[4,4,4,384]{3,2,1,0:T(4,128)(2,1)S(1)}, u32[]{:S(2)}, u32[]{:S(2)}) collective-permute-start(bf16[4,4,4,384]{3,2,1,0:T(4,128)(2,1)S(1)} %get-tuple-element.146), channel_id=1, source_target_pairs={{0,6},{1,7},{8,14},{9,15},{16,22},{17,23},{24,30},{25,31}} | collective-permute-start | bytes 147464 | tf_op jit(solution)/shard_map/ppermute | solution.py:13
  55.9 2.5 %collective-permute-start.4 = (bf16[4,4,4,384]{3,2,1,0:T(4,128)(2,1)}, bf16[4,4,4,384]{3,2,1,0:T(4,128)(2,1)}, u32[]{:S(2)}, u32[]{:S(2)}) collective-permute-start(bf16[4,4,4,384]{3,2,1,0:T(4,128)(2,1)} %get-tuple-element.147), channel_id=1, source_target_pairs={{0,2},{2,4},{4,6},{1,3},{3,5},{5,7},{8,10},{10,12},{12,14},{9,11},... | collective-permute-start | bytes 147464 | tf_op jit(solution)/shard_map/ppermute | solution.py:13
  61.9 5.9 %collective-permute-start.5 = (bf16[4,16,4,384]{3,2,1,0:T(4,128)(2,1)S(1)}, bf16[4,16,4,384]{3,2,1,0:T(4,128)(2,1)}, u32[]{:S(2)}, u32[]{:S(2)}) collective-permute-start(bf16[4,16,4,384]{3,2,1,0:T(4,128)(2,1)S(1)} %get-tuple-element.152), channel_id=1, source_target_pairs={{0,2},{2,4},{4,6},{1,3},{3,5},{5,7},{8,10},{10,12},{12,14},{9,11},... | collective-permute-start | bytes 589832 | tf_op jit(solution)/shard_map/ppermute | solution.py:13
  67.7 2.1 %dynamic-slice_select_fusion = bf16[4,4,24,384]{3,2,1,0:T(8,128)(2,1)S(1)} fusion(bf16[4,4,24,384]{3,2,1,0:T(8,128)(2,1)S(1)} %collective-permute-done.3, bf16[4,24,32,384]{3,2,1,0:T(8,128)(2,1)S(1)} %constant_dynamic-update-slice_fusion.4, s32[]{:T(128)} %bitcast.10, s32[]{:T(128)} %bitcast.11, pred[]{:T(512)} %and_reduce_fusion.1), kind=kLoop, calls=%fused_computation.60 | loop fusion | flops 147456 | bytes 884745 | tf_op jit(solution)/shard_map/select.9
  69.8 2.5 %scatter.29 = bf16[4,24,32,384]{3,2,1,0:T(8,128)(2,1)S(1)} dynamic-update-slice(bf16[4,24,32,384]{3,2,1,0:T(8,128)(2,1)S(1)} %constant_dynamic-update-slice_fusion.4, bf16[4,4,24,384]{3,2,1,0:T(8,128)(2,1)S(1)} %dynamic-slice_select_fusion, s32[]{:T(128)} %constant.277.clone.1, s32[]{:T(128)} %bitcast.10, s32[]{:T(128)} %bitcast.11, s32[]{:T(128)} %constant.277.clone.1) | dynamic-update-slice | bytes 589828 | tf_op jit(solution)/shard_map/scatter | solution.py:111
  73.9 3.3 %dynamic-slice_select_fusion.1 = bf16[4,4,4,384]{3,2,1,0:T(4,128)(2,1)} fusion(bf16[4,4,4,384]{3,2,1,0:T(4,128)(2,1)} %collective-permute-done.4, bf16[4,24,32,384]{3,2,1,0:T(8,128)(2,1)S(1)} %scatter.29, s32[]{:T(128)} %bitcast.12, s32[]{:T(128)} %bitcast.13, pred[]{:T(512)} %and_reduce_fusion), kind=kLoop, calls=%fused_computation.68 | loop fusion | flops 24576 | bytes 147465 | tf_op jit(solution)/shard_map/select.10
  77.2 2.2 %scatter.30 = bf16[4,24,32,384]{3,2,1,0:T(8,128)(2,1)S(1)} dynamic-update-slice(bf16[4,24,32,384]{3,2,1,0:T(8,128)(2,1)S(1)} %scatter.29, bf16[4,4,4,384]{3,2,1,0:T(4,128)(2,1)} %dynamic-slice_select_fusion.1, s32[]{:T(128)} %constant.277.clone.1, s32[]{:T(128)} %bitcast.12, s32[]{:T(128)} %bitcast.13, s32[]{:T(128)} %constant.277.clone.1) | dynamic-update-slice | bytes 98308 | tf_op jit(solution)/shard_map/scatter | solution.py:111
  81.5 8.3 %collective-permute-done.8 = bf16[4,4,24,384]{3,2,1,0:T(8,128)(2,1)S(1)} collective-permute-done((bf16[4,4,24,384]{3,2,1,0:T(8,128)(2,1)S(1)}, bf16[4,4,24,384]{3,2,1,0:T(8,128)(2,1)S(1)}, u32[]{:S(2)}, u32[]{:S(2)}) %collective-permute-start.8) | collective-permute-done | bytes 294944 | tf_op jit(solution)/shard_map/ppermute | solution.py:13
  92.4 2.2 %fusion.7 = bf16[4,24,32,384]{3,2,1,0:T(8,128)(2,1)S(1)} fusion(bf16[4,24,32,384]{3,2,1,0:T(8,128)(2,1)S(1)} %constant_dynamic-update-slice_fusion, f32[384]{0:T(512)} %param.25, f32[4,24,32]{2,1,0:T(8,128)S(1)} %add_rsqrt_fusion), kind=kLoop, calls=%fused_computation.9 | loop fusion | flops 9437184 | bytes 4732416 | tf_op jit(solution)/shard_map/convert_element_type | solution.py:19
  96.1 4.5 %fusion.23 = (bf16[2,24,32,384]{3,2,1,0:T(8,128)(2,1)S(1)}, bf16[2,24,32,384]{3,2,1,0:T(8,128)(2,1)S(1)}, bf16[2,24,32,384]{3,2,1,0:T(8,128)(2,1)}, bf16[2,24,32...) fusion(bf16[4,26,34,384]{3,2,1,0:T(8,128)(2,1)S(1)} %pad_select, ...), kind=kLoop, calls=%fused_computation.96 | loop fusion | bytes 18874368 | tf_op jit(solution)/shard_map/slice | solution.py:30
  100.6 6.3 %fusion.22 = (bf16[2,24,32,384]{3,2,1,0:T(8,128)(2,1)}, bf16[2,24,32,384]{3,2,1,0:T(8,128)(2,1)}, bf16[2,24,32,384]{3,2,1,0:T(8,128)(2,1)}, bf16[2,24,32,384]{3,...) fusion(bf16[4,26,34,384]{3,2,1,0:T(8,128)(2,1)S(1)} %pad_select, ...), kind=kLoop, calls=%fused_computation.95 | loop fusion | bytes 44826624 | tf_op jit(solution)/shard_map/slice | solution.py:30
  106.9 3.4 %pad_maximum_fusion = (bf16[2,24,32,1152]{3,2,1,0:T(8,128)(2,1)S(1)}, bf16[2,24,32,1152]{3,2,1,0:T(8,128)(2,1)S(1)}) fusion(bf16[2,24,32,384]{3,2,1,0:T(8,128)(2,1)} %get-tuple-element.134, bf16[2,24,32,384]{3,2,1,0:T(8,128)(2,1)} %get-tuple-element.135, bf16[2,24,32,384]{3,2,1,0:T(8,128)(2,1)} %get-tuple-element.136, ...), kind=kLoop, calls=%fused_computation.10 | loop fusion | flops 21233664 | bytes 14155776 | tf_op jit(solution)/shard_map/concatenate | solution.py:29
  110.3 2.1 %fusion.31 = f32[1536,384]{1,0:T(8,128)S(1)} fusion(bf16[1536,1152]{1,0:T(8,128)(2,1)S(1)} %bitcast.69, bf16[1152,384]{1,0:T(8,128)(2,1)S(1)} %bitcast.80), kind=kOutput, calls=%fused_computation.104 | convolution fusion | flops 1358954496 | bytes 6782976 | tf_op jit(solution)/shard_map/dot_general | solution.py:33
  112.5 3.6 %convolution_add_fusion.7 = f32[1536,384]{1,0:T(8,128)} fusion(f32[1536,384]{1,0:T(8,128)S(1)} %fusion.31, bf16[1536,1152]{1,0:T(8,128)(2,1)S(1)} %bitcast.65, bf16[1152,384]{1,0:T(8,128)(2,1)S(1)} %bitcast.79), kind=kOutput, calls=%fused_computation.27 | convolution fusion | flops 1359544320 | bytes 9142272 | tf_op jit(solution)/shard_map/dot_general | solution.py:33
  116.1 1.9 %pad_maximum_fusion.8 = bf16[2,24,32,1152]{3,2,1,0:T(8,128)(2,1)} fusion(bf16[2,24,32,384]{3,2,1,0:T(8,128)(2,1)S(1)} %copy-done.3, bf16[2,24,32,384]{3,2,1,0:T(8,128)(2,1)S(1)} %copy-done.4, bf16[2,24,32,384]{3,2,1,0:T(8,128)(2,1)S(1)} %copy-done.2), kind=kLoop, calls=%fused_computation.18 | loop fusion | flops 10616832 | bytes 7077888 | tf_op jit(solution)/shard_map/concatenate | solution.py:29
  119.2 3.9 %convolution_add_fusion.6 = f32[1536,384]{1,0:T(8,128)S(1)} fusion(f32[1536,384]{1,0:T(8,128)} %convolution_add_fusion.7, bf16[1536,1152]{1,0:T(8,128)(2,1)S(1)} %bitcast.66, bf16[1152,384]{1,0:T(8,128)(2,1)S(1)} %bitcast.78), kind=kOutput, calls=%fused_computation.26 | convolution fusion | flops 1359544320 | bytes 9142272 | tf_op jit(solution)/shard_map/dot_general | solution.py:33
  123.2 2.2 %convolution_add_fusion.5 = f32[1536,384]{1,0:T(8,128)S(1)} fusion(f32[1536,384]{1,0:T(8,128)S(1)} %convolution_add_fusion.6, bf16[1536,1152]{1,0:T(8,128)(2,1)S(1)} %bitcast.62, bf16[1152,384]{1,0:T(8,128)(2,1)S(1)} %bitcast.77), kind=kOutput, calls=%fused_computation.25 | convolution fusion | flops 1359544320 | bytes 9142272 | tf_op jit(solution)/shard_map/dot_general | solution.py:33
  126.5 2.2 %convolution_add_fusion.4 = f32[1536,384]{1,0:T(8,128)S(1)} fusion(f32[1536,384]{1,0:T(8,128)S(1)} %convolution_add_fusion.5, bf16[1536,1152]{1,0:T(8,128)(2,1)S(1)} %bitcast.67, bf16[1152,384]{1,0:T(8,128)(2,1)S(1)} %bitcast.76), kind=kOutput, calls=%fused_computation.24 | convolution fusion | flops 1359544320 | bytes 9142272 | tf_op jit(solution)/shard_map/dot_general | solution.py:33
  128.7 2.1 %convolution_add_fusion.3 = f32[1536,384]{1,0:T(8,128)S(1)} fusion(f32[1536,384]{1,0:T(8,128)S(1)} %convolution_add_fusion.4, bf16[1536,1152]{1,0:T(8,128)(2,1)S(1)} %bitcast.63, bf16[1152,384]{1,0:T(8,128)(2,1)S(1)} %bitcast.75), kind=kOutput, calls=%fused_computation.23 | convolution fusion | flops 1359544320 | bytes 9142272 | tf_op jit(solution)/shard_map/dot_general | solution.py:33
  132.0 2.2 %convolution_add_fusion.2 = f32[1536,384]{1,0:T(8,128)S(1)} fusion(f32[1536,384]{1,0:T(8,128)S(1)} %convolution_add_fusion.3, bf16[1536,1152]{1,0:T(8,128)(2,1)S(1)} %bitcast.68, bf16[1152,384]{1,0:T(8,128)(2,1)S(1)} %bitcast.74), kind=kOutput, calls=%fused_computation.22 | convolution fusion | flops 1359544320 | bytes 9142272 | tf_op jit(solution)/shard_map/dot_general | solution.py:33
  134.2 2.1 %convolution_add_fusion.1 = f32[1536,384]{1,0:T(8,128)S(1)} fusion(f32[1536,384]{1,0:T(8,128)S(1)} %convolution_add_fusion.2, bf16[1536,1152]{1,0:T(8,128)(2,1)S(1)} %bitcast.64, bf16[1152,384]{1,0:T(8,128)(2,1)S(1)} %bitcast.73), kind=kOutput, calls=%fused_computation.21 | convolution fusion | flops 1359544320 | bytes 9142272 | tf_op jit(solution)/shard_map/dot_general | solution.py:33
  136.4 2.1 %convolution_add_fusion = f32[1536,384]{1,0:T(8,128)S(1)} fusion(f32[1536,384]{1,0:T(8,128)S(1)} %convolution_add_fusion.1, bf16[1536,1152]{1,0:T(8,128)(2,1)S(1)} %bitcast.70, bf16[1152,384]{1,0:T(8,128)(2,1)S(1)} %bitcast.72), kind=kOutput, calls=%fused_computation.20 | convolution fusion | flops 1359544320 | bytes 9142272 | tf_op jit(solution)/shard_map/dot_general | solution.py:33
  143.0 4.5 %collective-permute-start.12 = (bf16[2,4,4,384]{3,2,1,0:T(4,128)(2,1)S(1)}, bf16[2,4,4,384]{3,2,1,0:T(4,128)(2,1)S(1)}, u32[]{:S(2)}, u32[]{:S(2)}) collective-permute-start(bf16[2,4,4,384]{3,2,1,0:T(4,128)(2,1)S(1)} %get-tuple-element.140), channel_id=1, source_target_pairs={{0,2},{2,4},{4,6},{1,3},{3,5},{5,7},{8,10},{10,12},{12,14},{9,11},... | collective-permute-start | bytes 73736 | tf_op jit(solution)/shard_map/ppermute | solution.py:13
  147.6 1.9 %collective-permute-start.13 = (bf16[2,16,4,384]{3,2,1,0:T(4,128)(2,1)S(1)}, bf16[2,16,4,384]{3,2,1,0:T(4,128)(2,1)S(1)}, u32[]{:S(2)}, u32[]{:S(2)}) collective-permute-start(bf16[2,16,4,384]{3,2,1,0:T(4,128)(2,1)S(1)} %get-tuple-element.143), channel_id=1, source_target_pairs={{0,2},{2,4},{4,6},{1,3},{3,5},{5,7},{8,10},{10,12},{12,14},{9,11},... | collective-permute-start | bytes 294920 | tf_op jit(solution)/shard_map/ppermute | solution.py:13
  150.8 6.9 %collective-permute-start.11 = (bf16[2,4,24,384]{3,2,1,0:T(8,128)(2,1)S(1)}, bf16[2,4,24,384]{3,2,1,0:T(8,128)(2,1)S(1)}, u32[]{:S(2)}, u32[]{:S(2)}) collective-permute-start(bf16[2,4,24,384]{3,2,1,0:T(8,128)(2,1)S(1)} %get-tuple-element.141), channel_id=1, source_target_pairs={{0,4},{2,6},{1,5},{3,7},{8,12},{10,14},{9,13},{11,15},{16,20},{18,... | collective-permute-start | bytes 442376 | tf_op jit(solution)/shard_map/ppermute | solution.py:13
  160.4 7.4 %collective-permute-done.16 = bf16[2,4,24,384]{3,2,1,0:T(8,128)(2,1)S(1)} collective-permute-done((bf16[2,4,24,384]{3,2,1,0:T(8,128)(2,1)S(1)}, bf16[2,4,24,384]{3,2,1,0:T(8,128)(2,1)S(1)}, u32[]{:S(2)}, u32[]{:S(2)}) %collective-permute-start.16) | collective-permute-done | bytes 147488 | tf_op jit(solution)/shard_map/ppermute | solution.py:13
  167.7 2.1 %fusion.12 = bf16[1,2,16,24,384]{4,3,2,1,0:T(8,128)(2,1)} fusion(f32[16,24]{1,0:T(8,128)S(1)} %get-tuple-element.154, f32[16,24]{1,0:T(8,128)S(1)} %get-tuple-element.155, bf16[2,4,4,384]{3,2,1,0:T(4,128)(2,1)S(1)} %collective-permute-done.17, f32[16]{0:T(128)S(1)} %get-tuple-element.179, bf16[2,4,24,384]{3,2,1,0:T(8,128)(2,1)S(1)} %collective-permute-done.16, ...), kind=kLoop, calls=%fused_computation.57 | loop fusion | flops 7962624 | bytes 1777472 | tf_op jit(solution)/shard_map/broadcast_in_dim | solution.py:163
  (101 shorter events, 36.5 us)
Async XLA Ops:
  0.0 21.6 %copy-start.18 = (s32[4]{0:T(128)S(1)}, s32[4]{0:T(128)}, u32[]{:S(2)}) copy-start(s32[4]{0:T(128)} %constant.284.clone.1) | copy-start | bytes 52
  0.0 22.3 %copy-start.17 = (s32[4]{0:T(128)S(1)}, s32[4]{0:T(128)}, u32[]{:S(2)}) copy-start(s32[4]{0:T(128)} %constant.287.clone.1) | copy-start | bytes 52
  0.0 16.5 %collective-permute-start = (bf16[1,2,16,24,384]{4,3,2,1,0:T(8,128)(2,1)}, bf16[1,2,16,24,384]{4,3,2,1,0:T(8,128)(2,1)S(1)}, u32[]{:S(2)}, u32[]{:S(2)}) collective-permute-start(bf16[1,2,16,24,384]{4,3,2,1,0:T(8,128)(2,1)} %param.22), channel_id=1, source_target_pairs={{0,8},{8,0},{16,24},{24,16},{1,9},{9,1},{17,25},{25,17},{2,10},{10... | collective-permute-start | bytes 1769480 | tf_op jit(solution)/shard_map/ppermute | solution.py:127
  18.0 27.2 %collective-permute-start.1 = (bf16[2,2,16,24,384]{4,3,2,1,0:T(8,128)(2,1)S(1)}, bf16[2,2,16,24,384]{4,3,2,1,0:T(8,128)(2,1)S(1)}, u32[]{:S(2)}, u32[]{:S(2)}) collective-permute-start(bf16[2,2,16,24,384]{4,3,2,1,0:T(8,128)(2,1)S(1)} %maximum_select_fusion.1), channel_id=1, source_target_pairs={{0,16},{8,24},{16,0},{24,8},{1,17},{9,25},{17,1},{25,9},{2,18},{10... | collective-permute-start | bytes 3538952 | tf_op jit(solution)/shard_map/ppermute | solution.py:127
  46.9 15.0 %collective-permute-start.3 = (bf16[4,4,24,384]{3,2,1,0:T(8,128)(2,1)S(1)}, bf16[4,4,24,384]{3,2,1,0:T(8,128)(2,1)S(1)}, u32[]{:S(2)}, u32[]{:S(2)}) collective-permute-start(bf16[4,4,24,384]{3,2,1,0:T(8,128)(2,1)S(1)} %get-tuple-element.150), channel_id=1, source_target_pairs={{0,4},{2,6},{1,5},{3,7},{8,12},{10,14},{9,13},{11,15},{16,20},{18,... | collective-permute-start | bytes 884744 | tf_op jit(solution)/shard_map/ppermute | solution.py:13
  52.1 8.4 %collective-permute-start.2 = (bf16[4,4,4,384]{3,2,1,0:T(4,128)(2,1)S(1)}, bf16[4,4,4,384]{3,2,1,0:T(4,128)(2,1)S(1)}, u32[]{:S(2)}, u32[]{:S(2)}) collective-permute-start(bf16[4,4,4,384]{3,2,1,0:T(4,128)(2,1)S(1)} %get-tuple-element.146), channel_id=1, source_target_pairs={{0,6},{1,7},{8,14},{9,15},{16,22},{17,23},{24,30},{25,31}} | collective-permute-start | bytes 147464 | tf_op jit(solution)/shard_map/ppermute | solution.py:13
  54.6 36.3 %collective-permute-start.9 = (bf16[4,4,4,384]{3,2,1,0:T(4,128)(2,1)}, bf16[4,4,4,384]{3,2,1,0:T(4,128)(2,1)}, u32[]{:S(2)}, u32[]{:S(2)}) collective-permute-start(bf16[4,4,4,384]{3,2,1,0:T(4,128)(2,1)} %get-tuple-element.145), channel_id=1, source_target_pairs={{6,0},{7,1},{14,8},{15,9},{22,16},{23,17},{30,24},{31,25}} | collective-permute-start | bytes 147464 | tf_op jit(solution)/shard_map/ppermute | solution.py:13
  55.9 16.4 %collective-permute-start.4 = (bf16[4,4,4,384]{3,2,1,0:T(4,128)(2,1)}, bf16[4,4,4,384]{3,2,1,0:T(4,128)(2,1)}, u32[]{:S(2)}, u32[]{:S(2)}) collective-permute-start(bf16[4,4,4,384]{3,2,1,0:T(4,128)(2,1)} %get-tuple-element.147), channel_id=1, source_target_pairs={{0,2},{2,4},{4,6},{1,3},{3,5},{5,7},{8,10},{10,12},{12,14},{9,11},... | collective-permute-start | bytes 147464 | tf_op jit(solution)/shard_map/ppermute | solution.py:13
  58.4 22.3 %collective-permute-start.7 = (bf16[4,4,4,384]{3,2,1,0:T(4,128)(2,1)}, bf16[4,4,4,384]{3,2,1,0:T(4,128)(2,1)}, u32[]{:S(2)}, u32[]{:S(2)}) collective-permute-start(bf16[4,4,4,384]{3,2,1,0:T(4,128)(2,1)} %get-tuple-element.148), channel_id=1, source_target_pairs={{2,0},{4,2},{6,4},{3,1},{5,3},{7,5},{10,8},{12,10},{14,12},{11,9},... | collective-permute-start | bytes 147464 | tf_op jit(solution)/shard_map/ppermute | solution.py:13
  60.5 20.0 %collective-permute-start.6 = (bf16[4,16,4,384]{3,2,1,0:T(4,128)(2,1)S(1)}, bf16[4,16,4,384]{3,2,1,0:T(4,128)(2,1)S(1)}, u32[]{:S(2)}, u32[]{:S(2)}) collective-permute-start(bf16[4,16,4,384]{3,2,1,0:T(4,128)(2,1)S(1)} %get-tuple-element.151), channel_id=1, source_target_pairs={{2,0},{4,2},{6,4},{3,1},{5,3},{7,5},{10,8},{12,10},{14,12},{11,9},... | collective-permute-start | bytes 589832 | tf_op jit(solution)/shard_map/ppermute | solution.py:13
  61.9 17.5 %collective-permute-start.5 = (bf16[4,16,4,384]{3,2,1,0:T(4,128)(2,1)S(1)}, bf16[4,16,4,384]{3,2,1,0:T(4,128)(2,1)}, u32[]{:S(2)}, u32[]{:S(2)}) collective-permute-start(bf16[4,16,4,384]{3,2,1,0:T(4,128)(2,1)S(1)} %get-tuple-element.152), channel_id=1, source_target_pairs={{0,2},{2,4},{4,6},{1,3},{3,5},{5,7},{8,10},{10,12},{12,14},{9,11},... | collective-permute-start | bytes 589832 | tf_op jit(solution)/shard_map/ppermute | solution.py:13
  72.4 17.4 %collective-permute-start.8 = (bf16[4,4,24,384]{3,2,1,0:T(8,128)(2,1)S(1)}, bf16[4,4,24,384]{3,2,1,0:T(8,128)(2,1)S(1)}, u32[]{:S(2)}, u32[]{:S(2)}) collective-permute-start(bf16[4,4,24,384]{3,2,1,0:T(8,128)(2,1)S(1)} %get-tuple-element.149), channel_id=1, source_target_pairs={{4,0},{6,2},{5,1},{7,3},{12,8},{14,10},{13,9},{15,11},{20,16},{22,... | collective-permute-start | bytes 884744 | tf_op jit(solution)/shard_map/ppermute | solution.py:13
  106.9 3.4 %copy-start.14 = (bf16[1,1,3,384,384]{4,3,2,1,0:T(8,128)(2,1)S(1)}, bf16[1,1,3,384,384]{4,3,2,1,0:T(8,128)(2,1)}, u32[]{:S(2)}) copy-start(bf16[1,1,3,384,384]{4,3,2,1,0:T(8,128)(2,1)} %get-tuple-element.108) | copy-start | bytes 2654212
  110.3 2.1 %copy-start.13 = (bf16[1,1,3,384,384]{4,3,2,1,0:T(8,128)(2,1)S(1)}, bf16[1,1,3,384,384]{4,3,2,1,0:T(8,128)(2,1)}, u32[]{:S(2)}) copy-start(bf16[1,1,3,384,384]{4,3,2,1,0:T(8,128)(2,1)} %get-tuple-element.107) | copy-start | bytes 2654212
  112.5 3.7 %copy-start.2 = (bf16[2,24,32,384]{3,2,1,0:T(8,128)(2,1)S(1)}, bf16[2,24,32,384]{3,2,1,0:T(8,128)(2,1)}, u32[]{:S(2)}) copy-start(bf16[2,24,32,384]{3,2,1,0:T(8,128)(2,1)} %get-tuple-element.110) | copy-start | bytes 3538948
  112.5 3.7 %copy-start.3 = (bf16[2,24,32,384]{3,2,1,0:T(8,128)(2,1)S(1)}, bf16[2,24,32,384]{3,2,1,0:T(8,128)(2,1)}, u32[]{:S(2)}) copy-start(bf16[2,24,32,384]{3,2,1,0:T(8,128)(2,1)} %get-tuple-element.111) | copy-start | bytes 3538948
  112.5 3.6 %copy-start.4 = (bf16[2,24,32,384]{3,2,1,0:T(8,128)(2,1)S(1)}, bf16[2,24,32,384]{3,2,1,0:T(8,128)(2,1)}, u32[]{:S(2)}) copy-start(bf16[2,24,32,384]{3,2,1,0:T(8,128)(2,1)} %get-tuple-element.112) | copy-start | bytes 3538948
  119.2 3.9 %copy-start.11 = (bf16[1,1,3,384,384]{4,3,2,1,0:T(8,128)(2,1)S(1)}, bf16[1,1,3,384,384]{4,3,2,1,0:T(8,128)(2,1)}, u32[]{:S(2)}) copy-start(bf16[1,1,3,384,384]{4,3,2,1,0:T(8,128)(2,1)} %get-tuple-element.105) | copy-start | bytes 2654212
  126.5 2.2 %copy-start.9 = (bf16[1,1,3,384,384]{4,3,2,1,0:T(8,128)(2,1)S(1)}, bf16[1,1,3,384,384]{4,3,2,1,0:T(8,128)(2,1)}, u32[]{:S(2)}) copy-start(bf16[1,1,3,384,384]{4,3,2,1,0:T(8,128)(2,1)} %get-tuple-element.103) | copy-start | bytes 2654212
  132.0 2.2 %copy-start.7 = (bf16[1,1,3,384,384]{4,3,2,1,0:T(8,128)(2,1)S(1)}, bf16[1,1,3,384,384]{4,3,2,1,0:T(8,128)(2,1)}, u32[]{:S(2)}) copy-start(bf16[1,1,3,384,384]{4,3,2,1,0:T(8,128)(2,1)} %get-tuple-element.109) | copy-start | bytes 2654212
  134.2 2.1 %copy-start.5 = (bf16[2,24,32,1152]{3,2,1,0:T(8,128)(2,1)S(1)}, bf16[2,24,32,1152]{3,2,1,0:T(8,128)(2,1)}, u32[]{:S(2)}) copy-start(bf16[2,24,32,1152]{3,2,1,0:T(8,128)(2,1)} %pad_maximum_fusion.8) | copy-start | bytes 10616836
  134.2 2.2 %copy-start.6 = (bf16[1,1,3,384,384]{4,3,2,1,0:T(8,128)(2,1)S(1)}, bf16[1,1,3,384,384]{4,3,2,1,0:T(8,128)(2,1)}, u32[]{:S(2)}) copy-start(bf16[1,1,3,384,384]{4,3,2,1,0:T(8,128)(2,1)} %get-tuple-element.101) | copy-start | bytes 2654212
  136.4 2.1 %copy-start.16 = (f32[384]{0:T(512)S(1)}, f32[384]{0:T(512)}, u32[]{:S(2)}) copy-start(f32[384]{0:T(512)} %param.27) | copy-start | bytes 4612
  138.6 20.5 %copy-start.15 = (f32[24]{0:T(128)S(1)}, f32[24]{0:T(128)}, u32[]{:S(2)}) copy-start(f32[24]{0:T(128)} %get-tuple-element.182) | copy-start | bytes 292
  139.0 10.5 %collective-permute-start.10 = (bf16[2,4,4,384]{3,2,1,0:T(4,128)(2,1)S(1)}, bf16[2,4,4,384]{3,2,1,0:T(4,128)(2,1)S(1)}, u32[]{:S(2)}, u32[]{:S(2)}) collective-permute-start(bf16[2,4,4,384]{3,2,1,0:T(4,128)(2,1)S(1)} %get-tuple-element.137), channel_id=1, source_target_pairs={{0,6},{1,7},{8,14},{9,15},{16,22},{17,23},{24,30},{25,31}} | collective-permute-start | bytes 73736 | tf_op jit(solution)/shard_map/ppermute | solution.py:13
  140.3 10.5 %collective-permute-start.17 = (bf16[2,4,4,384]{3,2,1,0:T(4,128)(2,1)S(1)}, bf16[2,4,4,384]{3,2,1,0:T(4,128)(2,1)S(1)}, u32[]{:S(2)}, u32[]{:S(2)}) collective-permute-start(bf16[2,4,4,384]{3,2,1,0:T(4,128)(2,1)S(1)} %get-tuple-element.138), channel_id=1, source_target_pairs={{6,0},{7,1},{14,8},{15,9},{22,16},{23,17},{30,24},{31,25}} | collective-permute-start | bytes 73736 | tf_op jit(solution)/shard_map/ppermute | solution.py:13
  141.6 16.1 %collective-permute-start.15 = (bf16[2,4,4,384]{3,2,1,0:T(4,128)(2,1)S(1)}, bf16[2,4,4,384]{3,2,1,0:T(4,128)(2,1)S(1)}, u32[]{:S(2)}, u32[]{:S(2)}) collective-permute-start(bf16[2,4,4,384]{3,2,1,0:T(4,128)(2,1)S(1)} %get-tuple-element.139), channel_id=1, source_target_pairs={{2,0},{4,2},{6,4},{3,1},{5,3},{7,5},{10,8},{12,10},{14,12},{11,9},... | collective-permute-start | bytes 73736 | tf_op jit(solution)/shard_map/ppermute | solution.py:13
  143.0 16.1 %collective-permute-start.12 = (bf16[2,4,4,384]{3,2,1,0:T(4,128)(2,1)S(1)}, bf16[2,4,4,384]{3,2,1,0:T(4,128)(2,1)S(1)}, u32[]{:S(2)}, u32[]{:S(2)}) collective-permute-start(bf16[2,4,4,384]{3,2,1,0:T(4,128)(2,1)S(1)} %get-tuple-element.140), channel_id=1, source_target_pairs={{0,2},{2,4},{4,6},{1,3},{3,5},{5,7},{8,10},{10,12},{12,14},{9,11},... | collective-permute-start | bytes 73736 | tf_op jit(solution)/shard_map/ppermute | solution.py:13
  147.6 11.6 %collective-permute-start.13 = (bf16[2,16,4,384]{3,2,1,0:T(4,128)(2,1)S(1)}, bf16[2,16,4,384]{3,2,1,0:T(4,128)(2,1)S(1)}, u32[]{:S(2)}, u32[]{:S(2)}) collective-permute-start(bf16[2,16,4,384]{3,2,1,0:T(4,128)(2,1)S(1)} %get-tuple-element.143), channel_id=1, source_target_pairs={{0,2},{2,4},{4,6},{1,3},{3,5},{5,7},{8,10},{10,12},{12,14},{9,11},... | collective-permute-start | bytes 294920 | tf_op jit(solution)/shard_map/ppermute | solution.py:13
  149.5 9.6 %collective-permute-start.14 = (bf16[2,16,4,384]{3,2,1,0:T(4,128)(2,1)S(1)}, bf16[2,16,4,384]{3,2,1,0:T(4,128)(2,1)S(1)}, u32[]{:S(2)}, u32[]{:S(2)}) collective-permute-start(bf16[2,16,4,384]{3,2,1,0:T(4,128)(2,1)S(1)} %get-tuple-element.144), channel_id=1, source_target_pairs={{2,0},{4,2},{6,4},{3,1},{5,3},{7,5},{10,8},{12,10},{14,12},{11,9},... | collective-permute-start | bytes 294920 | tf_op jit(solution)/shard_map/ppermute | solution.py:13
  150.8 9.6 %collective-permute-start.11 = (bf16[2,4,24,384]{3,2,1,0:T(8,128)(2,1)S(1)}, bf16[2,4,24,384]{3,2,1,0:T(8,128)(2,1)S(1)}, u32[]{:S(2)}, u32[]{:S(2)}) collective-permute-start(bf16[2,4,24,384]{3,2,1,0:T(8,128)(2,1)S(1)} %get-tuple-element.141), channel_id=1, source_target_pairs={{0,4},{2,6},{1,5},{3,7},{8,12},{10,14},{9,13},{11,15},{16,20},{18,... | collective-permute-start | bytes 442376 | tf_op jit(solution)/shard_map/ppermute | solution.py:13
  157.7 10.0 %collective-permute-start.16 = (bf16[2,4,24,384]{3,2,1,0:T(8,128)(2,1)S(1)}, bf16[2,4,24,384]{3,2,1,0:T(8,128)(2,1)S(1)}, u32[]{:S(2)}, u32[]{:S(2)}) collective-permute-start(bf16[2,4,24,384]{3,2,1,0:T(8,128)(2,1)S(1)} %get-tuple-element.142), channel_id=1, source_target_pairs={{4,0},{6,2},{5,1},{7,3},{12,8},{14,10},{13,9},{15,11},{20,16},{22,... | collective-permute-start | bytes 442376 | tf_op jit(solution)/shard_map/ppermute | solution.py:13
  (5 other events, 6.5 us)
